TPU v7x, 256 devices: a whole 4x4x8 slice. The times are simulated.
256 devices in a mesh: ka: 32 (over z_lo, y, core), pa: 8 (over z_hi, x).
Axes of the slice: x: 4, y: 4, z: 8 (z_hi: 2, z_lo: 4; z = z_hi * 4 + z_lo), core: 2. Of those that a mesh axis runs over, the one named last changes fastest.
Arguments:
- previous: float32 [256, 256, 256], P('ka', None, 'pa'), may hold values from -6 to 6
- current: float32 [256, 256, 256], P('ka', None, 'pa'), may hold values from -6 to 6
- energies: float32 [256, 256, 256], P('ka', None, 'pa'), may hold values from -0.5 to 0.5
- valence: float32 [256, 256, 256], P('ka'), may hold values from -0.375 to 0.375
- conduction: float32 [256, 256, 256], P('ka', None, 'pa'), may hold values from -0.375 to 0.375
- kernel: float32 [256, 256, 256], P(None, 'ka', 'pa'), may hold values from 0.05 to 0.35
Outputs:
- next_one: float32 [256, 256, 256], P('ka', None, 'pa')
- next_two: float32 [256, 256, 256], P('ka', None, 'pa')
All inputs are finite; a program needn't handle non-finite values.
Results may differ from a plain program's by a relative error of at most 0.000096.
Values sent between devices are 32-bit elements; how exact they have to be, the bound alone decides.
No kernel may reach another device: no remote copies, remote signals or barrier semaphores. Data moves between devices by JAX's collectives and lax.ppermute only.
A program may use at most 64 MiB of HBM per device.

v0:
```python
import math
import jax
import jax.numpy as jnp
from jax import lax
from jax.sharding import PartitionSpec as P

KY = 16


def phase_tables(total):
    points = jnp.arange(total)
    wide = total // KY
    coarse = points // KY
    finer = points % KY
    turns = (coarse[:, None] * coarse[None, :] % wide).astype(jnp.float32) / wide
    turns = turns + (finer[:, None] * finer[None, :] % KY).astype(jnp.float32) / KY
    angles = 2.0 * math.pi * turns
    return (jnp.cos(angles), jnp.sin(angles))


def screen_owned(flattened, kernel, cosine_table, sine_table):
    highest = lax.Precision.HIGHEST
    total = kernel.shape[0]
    even = jnp.dot(cosine_table, flattened, precision=highest)
    odd = jnp.dot(sine_table, flattened, precision=highest)
    weights = kernel.reshape(total, kernel.shape[1] * kernel.shape[2])
    return (
        jnp.dot(cosine_table, weights * even, precision=highest)
        + jnp.dot(sine_table, weights * odd, precision=highest)
    ) / total


def kernel_product(field, valence, conduction, kernel, cosine_table, sine_table):
    highest = lax.Precision.HIGHEST
    total = kernel.shape[0]
    inner = jnp.einsum("kvc,kcn->kvn", field, conduction, precision=highest)
    pair_blocks = jnp.einsum("kvm,kvn->kmn", valence, inner, precision=highest)
    owned = lax.all_to_all(pair_blocks, "ka", split_axis=1, concat_axis=0, tiled=True)
    flattened = owned.reshape(total, owned.shape[1] * owned.shape[2])
    screened = screen_owned(flattened, kernel, cosine_table, sine_table).reshape(owned.shape)
    returned = lax.all_to_all(screened, "ka", split_axis=0, concat_axis=1, tiled=True)
    partial_rows = jnp.einsum("kmn,kcn->kmc", returned, conduction, precision=highest)
    return jnp.einsum("kvm,kmc->kvc", valence, partial_rows, precision=highest)


def on_device(previous, current, energies, valence, conduction, kernel):
    cosine_table, sine_table = phase_tables(kernel.shape[0])
    whole_current = lax.all_gather(current, "pa", axis=2, tiled=True)
    folded_term = kernel_product(
        whole_current, valence, conduction, kernel, cosine_table, sine_table
    )
    summed = lax.psum_scatter(folded_term, "pa", scatter_dimension=2, tiled=True)
    next_one = 2.0 * (energies * current + summed) - previous
    whole_next = lax.all_gather(next_one, "pa", axis=2, tiled=True)
    second_term = kernel_product(whole_next, valence, conduction, kernel, cosine_table, sine_table)
    second_sum = lax.psum_scatter(second_term, "pa", scatter_dimension=2, tiled=True)
    next_two = 2.0 * (energies * next_one + second_sum) - current
    return (next_one, next_two)


def solution(mesh):
    placed = (
        P("ka", None, "pa"),
        P("ka", None, "pa"),
        P("ka", None, "pa"),
        P("ka", None, None),
        P("ka", None, "pa"),
        P(None, "ka", "pa"),
    )
    return jax.shard_map(
        on_device,
        mesh=mesh,
        in_specs=placed,
        out_specs=(P("ka", None, "pa"), P("ka", None, "pa")),
        check_vma=False,
    )
```

profile of v0, /device:TPU:8, one launch (start us, length us, event | category | flops | bytes accessed | tf_op | source)
XLA Modules:
  0.0 477.2 jit_solution(5078884266012246509)
XLA Ops:
  7.2 0.7 all-gather.3.cloned.1.call-update
  7.9 81.5 %all-gather.3.cloned.1.call-done = f32[8,256,256]{1,2,0:T(8,128)} async-done(((f32[8,256,32]{1,2,0:T(8,128)}), f32[8,256,256]{1,2,0:T(8,128)}) %all-gather.3.cloned.1.call-update) | async-done | bytes 2097168 | tf_op jit(solution)/shard_map/all_gather | solution.py:48
  89.4 3.0 fusion.60
  92.4 1.3 convolution_bitcast_fusion.3
  94.1 1.2 reshape.71
  95.2 5.2 %all-to-all-start = ((f32[32,1,2048]{2,1,0:T(1,128)}), f32[32,1,2048]{2,1,0:T(1,128)S(1)}, u32[]{:S(2)}, u32[]{:S(2)}) async-start(f32[32,1,2048]{2,1,0:T(1,128)} %reshape.71), calls=%async_computation | async-start | bytes 524288 | tf_op jit(solution)/shard_map/all_to_all | solution.py:38
  100.8 1.8 copy.34
  102.6 7.3 %all-to-all-done = f32[32,1,2048]{2,1,0:T(1,128)S(1)} async-done(((f32[32,1,2048]{2,1,0:T(1,128)}), f32[32,1,2048]{2,1,0:T(1,128)S(1)}, u32[]{:S(2)}, u32[]{:S(2)}) %all-to-all-start) | async-done | bytes 262176 | tf_op jit(solution)/shard_map/all_to_all | solution.py:38
  109.8 0.6 broadcast.134
  110.4 1.2 reduce
  112.0 1.2 copy.33
  113.1 1.5 reshape.67
  114.7 1.6 convolution_multiply_fusion.2
  116.3 1.6 convolution_multiply_fusion.3
  117.8 1.7 fusion.19
  119.5 1.7 fusion.1
  121.2 0.4 copy.36
  121.6 1.2 reshape.73
  122.8 15.4 %all_to_all.66 = f32[32,1,2048]{2,1,0:T(1,128)S(1)} all-to-all(f32[32,1,2048]{2,1,0:T(1,128)} %reshape.73), channel_id=1, replica_groups=mesh['ka'=32,'pa'=8] {'ka'}, dimensions={0} | all-to-all | bytes 524288 | tf_op jit(solution)/shard_map/all_to_all | solution.py:41
  138.2 2.0 reduce.1
  140.2 1.3 reshape.74
  141.5 1.9 fusion.4
  143.4 3.5 convolution_bitcast_fusion.1
  146.9 92.0 %reduce-scatter.3.cloned.1.call-done = f32[8,256,32]{1,2,0:T(8,128)} async-done(((f32[8,256,256]{1,2,0:T(8,128)}), f32[8,256,32]{1,2,0:T(8,128)}) %reduce-scatter.3.cloned.1.call-update) | async-done | bytes 262160 | tf_op jit(solution)/shard_map/reduce_scatter | solution.py:52
  239.0 1.7 multiply_subtract_fusion.1
  240.8 73.1 %all-gather.5.cloned.1.call-done = f32[8,256,256]{1,2,0:T(8,128)} async-done(((f32[8,256,32]{1,2,0:T(8,128)}), f32[8,256,256]{1,2,0:T(8,128)}) %all-gather.5.cloned.1.call-update) | async-done | bytes 2097168 | tf_op jit(solution)/shard_map/all_gather | solution.py:54
  313.9 3.0 fusion.61
  316.8 2.0 convolution_bitcast_fusion.2
  318.9 1.4 copy.40
  320.2 1.2 reshape.75
  321.4 14.7 %all_to_all.67 = f32[32,1,2048]{2,1,0:T(1,128)S(1)} all-to-all(f32[32,1,2048]{2,1,0:T(1,128)} %reshape.75), channel_id=1, replica_groups=mesh['ka'=32,'pa'=8] {'ka'}, dimensions={0} | all-to-all | bytes 524288 | tf_op jit(solution)/shard_map/all_to_all | solution.py:38
  336.1 2.0 reduce.2
  338.1 1.3 reshape.76
  339.4 1.2 copy.42
  340.5 1.6 reshape.69
  342.1 2.5 convolution_multiply_fusion
  344.7 1.6 convolution_multiply_fusion.1
  346.2 1.7 fusion.16
  347.9 2.4 fusion
  350.3 1.4 copy.45
  351.7 1.2 reshape.77
  352.8 15.1 %all_to_all.68 = f32[32,1,2048]{2,1,0:T(1,128)S(1)} all-to-all(f32[32,1,2048]{2,1,0:T(1,128)} %reshape.77), channel_id=1, replica_groups=mesh['ka'=32,'pa'=8] {'ka'}, dimensions={0} | all-to-all | bytes 524288 | tf_op jit(solution)/shard_map/all_to_all | solution.py:41
  368.0 2.0 reduce.3
  369.9 1.3 reshape.78
  371.2 1.9 fusion.2
  373.1 3.5 convolution_bitcast_fusion
  376.6 92.1 %reduce-scatter.5.cloned.1.call-done = f32[8,256,32]{1,2,0:T(8,128)} async-done(((f32[8,256,256]{1,2,0:T(8,128)}), f32[8,256,32]{1,2,0:T(8,128)}) %reduce-scatter.5.cloned.1.call-update) | async-done | bytes 262160 | tf_op jit(solution)/shard_map/reduce_scatter | solution.py:56
  468.7 1.7 multiply_subtract_fusion
  (30 shorter events, 1.3 us)
Async XLA Ops:
  7.2 85.2 %copy-start = (f32[8,256,256]{2,1,0:T(8,128)S(1)}, f32[8,256,256]{2,1,0:T(8,128)}, u32[]{:S(2)}) copy-start(f32[8,256,256]{2,1,0:T(8,128)} %param.9) | copy-start | bytes 6291460
  7.2 82.2 %all-gather.3.cloned.1.call-start = ((), (), s32[]{:S(2)}) async-start(), calls=%async_computation.6 | async-start | bytes 2359296 | tf_op jit(solution)/shard_map/all_gather | solution.py:48
  95.2 14.6 %all-to-all-start = ((f32[32,1,2048]{2,1,0:T(1,128)}), f32[32,1,2048]{2,1,0:T(1,128)S(1)}, u32[]{:S(2)}, u32[]{:S(2)}) async-start(f32[32,1,2048]{2,1,0:T(1,128)} %reshape.71), calls=%async_computation | async-start | bytes 524288 | tf_op jit(solution)/shard_map/all_to_all | solution.py:38
  100.4 138.5 %reduce-scatter.3.cloned.1.call-start = ((), (), s32[]{:S(2)}) async-start(), calls=%async_computation.7 | async-start | bytes 2359296 | tf_op jit(solution)/shard_map/reduce_scatter | solution.py:52
  112.0 2.7 copy-start.8
  121.6 19.9 %copy-start.1 = (f32[8,256,32]{1,2,0:T(8,128)S(1)}, f32[8,256,32]{1,2,0:T(8,128)}, u32[]{:S(2)}) copy-start(f32[8,256,32]{1,2,0:T(8,128)} %param.10) | copy-start | bytes 786436
  146.8 92.1 %copy-start.2 = (f32[8,256,32]{1,2,0:T(8,128)S(1)}, f32[8,256,32]{1,2,0:T(8,128)}, u32[]{:S(2)}) copy-start(f32[8,256,32]{1,2,0:T(8,128)} %param.7) | copy-start | bytes 786436
  146.8 92.1 %copy-start.5 = (f32[8,256,32]{1,2,0:T(8,128)S(1)}, f32[8,256,32]{1,2,0:T(8,128)}, u32[]{:S(2)}) copy-start(f32[8,256,32]{1,2,0:T(8,128)} %param.8) | copy-start | bytes 786436
  146.8 92.1 %copy-start.7 = (f32[8,256,32]{1,2,0:T(8,128)S(1)}, f32[8,256,32]{1,2,0:T(8,128)}, u32[]{:S(2)}) copy-start(f32[8,256,32]{1,2,0:T(8,128)} %param.6) | copy-start | bytes 786436
  146.9 167.0 %all-gather.5.cloned.1.call-start = ((), (), s32[]{:S(2)}) async-start(), calls=%async_computation.8 | async-start | bytes 2359296 | tf_op jit(solution)/shard_map/all_gather | solution.py:54
  240.7 228.0 %reduce-scatter.5.cloned.1.call-start = ((), (), s32[]{:S(2)}) async-start(), calls=%async_computation.9 | async-start | bytes 2359296 | tf_op jit(solution)/shard_map/reduce_scatter | solution.py:56
  340.5 4.1 copy-start.9
  376.6 92.1 %copy-start.3 = (f32[8,256,32]{1,2,0:T(8,128)S(1)}, f32[8,256,32]{1,2,0:T(8,128)}, u32[]{:S(2)}) copy-start(f32[8,256,32]{1,2,0:T(8,128)} %param.7) | copy-start | bytes 786436
  376.6 92.1 %copy-start.4 = (f32[8,256,32]{1,2,0:T(8,128)S(1)}, f32[8,256,32]{1,2,0:T(8,128)}, u32[]{:S(2)}) copy-start(f32[8,256,32]{1,2,0:T(8,128)} %multiply_subtract_fusion.1) | copy-start | bytes 786436
  376.6 92.1 %copy-start.6 = (f32[8,256,32]{1,2,0:T(8,128)S(1)}, f32[8,256,32]{1,2,0:T(8,128)}, u32[]{:S(2)}) copy-start(f32[8,256,32]{1,2,0:T(8,128)} %param.8) | copy-start | bytes 786436
Sparse Core Ops, SparseCore 0:
  10.6 78.7 all-gather.2
  147.0 91.9 reduce-scatter.2
  242.2 71.6 all-gather.4
  376.7 91.9 reduce-scatter.4
where the time goes:
time: 481 us; the launch traced here: 477 us
  waiting for transfers between devices  347 us (72%)
  blocking collectives  45.3 us (9%)
  matrix products  34.5 us (7%)
  local copies, waits for them, and re-layouts  20.2 us (4%)
  between operations  14.2 us (3%)
  other arithmetic  10.6 us (2%)
  starting transfers between devices  5.63 us (1%)
    reduce_scatter x1, waiting for transfers between devices, on_device(): lax.psum_scatter(second_term, 'pa', scatter_dimension=2, tiled=True)  92.1 us
    reduce_scatter x1, waiting for transfers between devices, on_device(): lax.psum_scatter(folded_term, 'pa', scatter_dimension=2, tiled=True)  92 us
    all_gather x1, waiting for transfers between devices, on_device(): whole_current = lax.all_gather(current, 'pa', axis=2, tiled=True)  81.5 us
    all_gather x1, waiting for transfers between devices, on_device(): whole_next = lax.all_gather(next_one, 'pa', axis=2, tiled=True)  73.1 us
    all_to_all x2, blocking collectives, kernel_product(): lax.all_to_all(screened, 'ka', split_axis=0, concat_axis=1, tiled=True)  30.6 us
    all_to_all x1, blocking collectives, kernel_product(): lax.all_to_all(pair_blocks, 'ka', split_axis=1, concat_axis=0, tiled=True)  14.7 us
  transfers between devices with their start and end apart: 5, of which 5 were waited for; matrix products, arithmetic and copies ran while one was open for 0% of the time, Pallas kernels for 0%

commit v1 on v0

--- a/solution.py
+++ b/solution.py
@@ -51,7 +51,9 @@
     )
     summed = lax.psum_scatter(folded_term, "pa", scatter_dimension=2, tiled=True)
     next_one = 2.0 * (energies * current + summed) - previous
-    whole_next = lax.all_gather(next_one, "pa", axis=2, tiled=True)
+    whole_next = jnp.concatenate(
+        lax.all_to_all(jnp.stack([next_one] * lax.axis_size("pa")), "pa", 0, 0), axis=2
+    )
     second_term = kernel_product(whole_next, valence, conduction, kernel, cosine_table, sine_table)
     second_sum = lax.psum_scatter(second_term, "pa", scatter_dimension=2, tiled=True)
     next_two = 2.0 * (energies * next_one + second_sum) - current

time: 481 us -> 460 us (0.956)
  waiting for transfers between devices: 347 us -> 272 us
  blocking collectives: 45.3 us -> 100 us
    all_gather x1 -> x0, waiting for transfers between devices: 73.1 us -> none  [on_device(): whole_next = lax.all_gather(next_one, 'pa', axis=2, tiled=True)]
    all_to_all x0 -> x1, blocking collectives: none -> 51.1 us  [on_device(): lax.all_to_all(jnp.stack([next_one] * lax.axis_size('pa')), 'pa', 0, 0)]
  transfers between devices with their start and end apart: 5 -> 4, of which waited for: 5 -> 4; matrix products, arithmetic and copies ran while one was open for 0% -> 0% of each run, Pallas kernels for 0% -> 0%
where the time goes in v1:
time: 460 us; the launch traced here: 456 us
  waiting for transfers between devices  272 us (59%)
  blocking collectives  100 us (22%)
  matrix products  32.9 us (7%)
  local copies, waits for them, and re-layouts  21.2 us (5%)
  between operations  14.3 us (3%)
  other arithmetic  9.85 us (2%)
  starting transfers between devices  5.59 us (1%)
    reduce_scatter x1, waiting for transfers between devices, on_device(): lax.psum_scatter(folded_term, 'pa', scatter_dimension=2, tiled=True)  92 us
    reduce_scatter x1, waiting for transfers between devices, on_device(): lax.psum_scatter(second_term, 'pa', scatter_dimension=2, tiled=True)  90.1 us
    all_gather x1, waiting for transfers between devices, on_device(): whole_current = lax.all_gather(current, 'pa', axis=2, tiled=True)  81.5 us
    all_to_all x1, blocking collectives, on_device(): lax.all_to_all(jnp.stack([next_one] * lax.axis_size('pa')), 'pa', 0, 0)  51.1 us
    all_to_all x2, blocking collectives, kernel_product(): lax.all_to_all(screened, 'ka', split_axis=0, concat_axis=1, tiled=True)  30.6 us
    all_to_all x1, blocking collectives, kernel_product(): lax.all_to_all(pair_blocks, 'ka', split_axis=1, concat_axis=0, tiled=True)  18.5 us
    unnamed x30, local copies, waits for them, and re-layouts  9.31 us
  transfers between devices with their start and end apart: 4, of which 4 were waited for; matrix products, arithmetic and copies ran while one was open for 0% of the time, Pallas kernels for 0%

profile of v1, /device:TPU:8, one launch (start us, length us, event | category | flops | bytes accessed | tf_op | source)
XLA Modules:
  0.0 455.5 jit_solution(15434855989084327053)
XLA Ops:
  7.2 0.7 all-gather.2.cloned.1.call-update
  7.9 81.5 %all-gather.2.cloned.1.call-done = f32[8,256,256]{1,2,0:T(8,128)} async-done(((f32[8,256,32]{1,2,0:T(8,128)}), f32[8,256,256]{1,2,0:T(8,128)}) %all-gather.2.cloned.1.call-update) | async-done | bytes 2097168 | tf_op jit(solution)/shard_map/all_gather | solution.py:48
  89.4 3.0 fusion.60
  92.4 1.3 convolution_bitcast_fusion.3
  94.1 1.2 reshape.81
  95.2 5.2 %all-to-all-start = ((f32[32,1,2048]{2,1,0:T(1,128)}), f32[32,1,2048]{2,1,0:T(1,128)S(1)}, u32[]{:S(2)}, u32[]{:S(2)}) async-start(f32[32,1,2048]{2,1,0:T(1,128)} %reshape.81), calls=%async_computation | async-start | bytes 524288 | tf_op jit(solution)/shard_map/all_to_all | solution.py:38
  100.8 1.8 copy.37
  102.6 7.3 %all-to-all-done = f32[32,1,2048]{2,1,0:T(1,128)S(1)} async-done(((f32[32,1,2048]{2,1,0:T(1,128)}), f32[32,1,2048]{2,1,0:T(1,128)S(1)}, u32[]{:S(2)}, u32[]{:S(2)}) %all-to-all-start) | async-done | bytes 262176 | tf_op jit(solution)/shard_map/all_to_all | solution.py:38
  109.8 0.6 broadcast.136
  110.4 1.2 reduce
  112.0 1.2 copy.36
  113.2 1.5 reshape.75
  114.7 1.6 convolution_multiply_fusion.2
  116.3 1.6 convolution_multiply_fusion.3
  117.8 1.7 fusion.19
  119.5 1.7 fusion.1
  121.7 1.2 reshape.83
  122.8 15.4 %all_to_all.71 = f32[32,1,2048]{2,1,0:T(1,128)S(1)} all-to-all(f32[32,1,2048]{2,1,0:T(1,128)} %reshape.83), channel_id=1, replica_groups=mesh['ka'=32,'pa'=8] {'ka'}, dimensions={0} | all-to-all | bytes 524288 | tf_op jit(solution)/shard_map/all_to_all | solution.py:41
  138.3 2.0 reduce.1
  140.2 1.3 reshape.84
  141.5 1.9 fusion.4
  143.4 3.5 convolution_bitcast_fusion.1
  146.9 92.0 %reduce-scatter.3.cloned.1.call-done = f32[8,256,32]{1,2,0:T(8,128)} async-done(((f32[8,256,256]{1,2,0:T(8,128)}), f32[8,256,32]{1,2,0:T(8,128)}) %reduce-scatter.3.cloned.1.call-update) | async-done | bytes 262160 | tf_op jit(solution)/shard_map/reduce_scatter | solution.py:52
  239.0 1.0 multiply_subtract_fusion.1
  240.3 0.4 copy-done.2
  240.7 51.1 %all_to_all.72 = f32[8,8,256,32]{2,3,1,0:T(8,128)S(1)} all-to-all(f32[8,8,256,32]{2,3,1,0:T(8,128)S(1)} %stack.2), channel_id=1, replica_groups=mesh['ka'=32,'pa'=8] {'pa'}, dimensions={0} | all-to-all | bytes 4194304 | tf_op jit(solution)/shard_map/all_to_all | solution.py:55
  292.0 1.4 fusion.61
  293.4 2.0 convolution_bitcast_fusion.2
  295.4 1.4 copy.45
  296.8 1.2 reshape.85
  297.9 18.5 %all_to_all.73 = f32[32,1,2048]{2,1,0:T(1,128)S(1)} all-to-all(f32[32,1,2048]{2,1,0:T(1,128)} %reshape.85), channel_id=1, replica_groups=mesh['ka'=32,'pa'=8] {'ka'}, dimensions={0} | all-to-all | bytes 524288 | tf_op jit(solution)/shard_map/all_to_all | solution.py:38
  316.4 2.0 reduce.2
  318.4 1.3 reshape.86
  319.7 1.2 copy.47
  320.9 1.6 reshape.79
  322.4 2.5 convolution_multiply_fusion
  325.0 1.6 convolution_multiply_fusion.1
  326.6 1.7 fusion.16
  328.2 2.4 fusion
  330.6 1.4 copy.50
  332.0 1.2 reshape.87
  333.2 15.1 %all_to_all.74 = f32[32,1,2048]{2,1,0:T(1,128)S(1)} all-to-all(f32[32,1,2048]{2,1,0:T(1,128)} %reshape.87), channel_id=1, replica_groups=mesh['ka'=32,'pa'=8] {'ka'}, dimensions={0} | all-to-all | bytes 524288 | tf_op jit(solution)/shard_map/all_to_all | solution.py:41
  348.3 2.0 reduce.3
  350.3 1.3 reshape.88
  351.6 1.9 fusion.2
  353.4 3.5 convolution_bitcast_fusion
  356.9 90.1 %reduce-scatter.5.cloned.1.call-done = f32[8,256,32]{1,2,0:T(8,128)} async-done(((f32[8,256,256]{1,2,0:T(8,128)}), f32[8,256,32]{1,2,0:T(8,128)}) %reduce-scatter.5.cloned.1.call-update) | async-done | bytes 262160 | tf_op jit(solution)/shard_map/reduce_scatter | solution.py:58
  447.0 1.7 multiply_subtract_fusion
  (32 shorter events, 2.1 us)
Async XLA Ops:
  7.2 85.2 %copy-start = (f32[8,256,256]{2,1,0:T(8,128)S(1)}, f32[8,256,256]{2,1,0:T(8,128)}, u32[]{:S(2)}) copy-start(f32[8,256,256]{2,1,0:T(8,128)} %param.9) | copy-start | bytes 6291460
  7.2 82.2 %all-gather.2.cloned.1.call-start = ((), (), s32[]{:S(2)}) async-start(), calls=%async_computation.7 | async-start | bytes 2359296 | tf_op jit(solution)/shard_map/all_gather | solution.py:48
  95.2 14.6 %all-to-all-start = ((f32[32,1,2048]{2,1,0:T(1,128)}), f32[32,1,2048]{2,1,0:T(1,128)S(1)}, u32[]{:S(2)}, u32[]{:S(2)}) async-start(f32[32,1,2048]{2,1,0:T(1,128)} %reshape.81), calls=%async_computation | async-start | bytes 524288 | tf_op jit(solution)/shard_map/all_to_all | solution.py:38
  100.4 138.5 %reduce-scatter.3.cloned.1.call-start = ((), (), s32[]{:S(2)}) async-start(), calls=%async_computation.8 | async-start | bytes 2359296 | tf_op jit(solution)/shard_map/reduce_scatter | solution.py:52
  112.0 2.7 copy-start.9
  121.7 19.9 %copy-start.1 = (f32[8,256,32]{1,2,0:T(8,128)S(1)}, f32[8,256,32]{1,2,0:T(8,128)}, u32[]{:S(2)}) copy-start(f32[8,256,32]{1,2,0:T(8,128)} %param.10) | copy-start | bytes 786436
  146.8 92.1 %copy-start.4 = (f32[8,256,32]{1,2,0:T(8,128)S(1)}, f32[8,256,32]{1,2,0:T(8,128)}, u32[]{:S(2)}) copy-start(f32[8,256,32]{1,2,0:T(8,128)} %param.7) | copy-start | bytes 786436
  146.8 92.1 %copy-start.6 = (f32[8,256,32]{1,2,0:T(8,128)S(1)}, f32[8,256,32]{1,2,0:T(8,128)}, u32[]{:S(2)}) copy-start(f32[8,256,32]{1,2,0:T(8,128)} %param.8) | copy-start | bytes 786436
  146.9 92.1 %copy-start.8 = (f32[8,256,32]{1,2,0:T(8,128)S(1)}, f32[8,256,32]{1,2,0:T(8,128)}, u32[]{:S(2)}) copy-start(f32[8,256,32]{1,2,0:T(8,128)} %param.6) | copy-start | bytes 786436
  146.9 300.1 %reduce-scatter.5.cloned.1.call-start = ((), (), s32[]{:S(2)}) async-start(), calls=%async_computation.9 | async-start | bytes 2359296 | tf_op jit(solution)/shard_map/reduce_scatter | solution.py:58
  240.0 0.7 copy-start.2
  320.9 4.1 copy-start.10
  356.9 90.1 %copy-start.3 = (f32[8,256,32]{1,2,0:T(8,128)S(1)}, f32[8,256,32]{1,2,0:T(8,128)}, u32[]{:S(2)}) copy-start(f32[8,256,32]{1,2,0:T(8,128)} %copy-done.2) | copy-start | bytes 786436
  356.9 90.1 %copy-start.5 = (f32[8,256,32]{1,2,0:T(8,128)S(1)}, f32[8,256,32]{1,2,0:T(8,128)}, u32[]{:S(2)}) copy-start(f32[8,256,32]{1,2,0:T(8,128)} %param.7) | copy-start | bytes 786436
  356.9 90.1 %copy-start.7 = (f32[8,256,32]{1,2,0:T(8,128)S(1)}, f32[8,256,32]{1,2,0:T(8,128)}, u32[]{:S(2)}) copy-start(f32[8,256,32]{1,2,0:T(8,128)} %param.8) | copy-start | bytes 786436
Sparse Core Ops, SparseCore 0:
  10.6 78.7 all-gather.1
  147.0 91.9 reduce-scatter.2
  357.0 89.9 reduce-scatter.4
